TPU v7x, 256 devices: a whole 4x4x8 slice. The times are simulated.
256 devices in a mesh: row: 16 (over z, core), col: 8 (over x_hi, y), feat: 2 (over x_lo).
Axes of the slice: x: 4 (x_hi: 2, x_lo: 2; x = x_hi * 2 + x_lo), y: 4, z: 8, core: 2. Of those that a mesh axis runs over, the one named last changes fastest.
Arguments:
- features: bfloat16 [65536, 256], P(('col', 'row'), 'feat'), may hold values from -6 to 6
- tile_rows: int32 [16, 8, 256], P('row', 'col'), may hold values from 0 to 31, as said below
- tile_cols: int32 [16, 8, 256], P('row', 'col'), may hold values from 0 to 63
- tile_count: int32 [16, 8], P('row', 'col'), may hold values from 64 to 256, as said below
- tile_values: bfloat16 [16, 8, 256, 128, 128], P('row', 'col'), may hold values from -0.21875 to 0.21875
- weights: bfloat16 [256, 256], replicated, may hold values from -0.375 to 0.375
- cotangent: bfloat16 [65536, 256], P(('row', 'col'), 'feat'), may hold values from -6 to 6
Outputs:
- activated: bfloat16 [65536, 256], P(('row', 'col'), 'feat')
- feature_grad: bfloat16 [65536, 256], P(('col', 'row'), 'feat')
- weight_grad: float32 [256, 256], P('feat')
Inputs may be any that keep to these rules, and one draw needn't show every extreme that they name: `tile_rows`: block rows of a cell, unevenly loaded. `tile_count`: some cell has all 256 slots live.
All inputs are finite; a program needn't handle non-finite values.
Results may differ from a plain program's by a relative error of at most 0.027.
Values may be sent and summed in bfloat16 or wider, within the bound.
A program may use at most 128 MiB of HBM per device.

v0:
```python
import jax
import jax.numpy as jnp
from jax import lax
from jax.sharding import PartitionSpec as P


def shards(features, tile_rows, tile_cols, tile_count, tile_values, weights, cotangent):
    width = tile_values.shape[-1]
    slots = tile_values.shape[2]
    local_tiles = tile_values[0, 0]
    block_rows = tile_rows[0, 0]
    block_cols = tile_cols[0, 0]
    live_mask = (jnp.arange(slots) < tile_count[0, 0]).astype(jnp.float32)
    n_rowdev = lax.axis_size("row")
    n_coldev = lax.axis_size("col")
    local_blocks = features.shape[0] // width
    feat_half = features.shape[1]
    feat_index = lax.axis_index("feat")
    row_blocks = local_blocks * n_coldev
    col_blocks = local_blocks * n_rowdev
    node_total = features.shape[0] * n_rowdev * n_coldev
    panel = lax.all_gather(features, "row", axis=0, tiled=True)
    gathered = panel.reshape(col_blocks, width, feat_half)[block_cols]
    products = jnp.einsum("tij,tjf->tif", local_tiles, gathered, preferred_element_type=jnp.float32)
    products = products * live_mask[:, None, None]
    partial_value = (
        jnp.zeros((row_blocks, width, feat_half), jnp.float32).at[block_rows].add(products)
    )
    summed = lax.psum_scatter(
        partial_value.reshape(row_blocks * width, feat_half).astype(jnp.bfloat16),
        "col",
        scatter_dimension=0,
        tiled=True,
    )
    weight_rows = lax.dynamic_slice_in_dim(weights, feat_index * feat_half, feat_half, 0)
    mix_term = jnp.dot(summed, weight_rows, preferred_element_type=jnp.float32)
    hidden = lax.psum_scatter(
        mix_term.astype(jnp.bfloat16), "feat", scatter_dimension=1, tiled=True
    ).astype(jnp.float32)
    negative = jnp.minimum(hidden, 0.0)
    activated = jnp.where(hidden > 0, hidden, jnp.expm1(negative)).astype(jnp.bfloat16)
    slope_factor = jnp.where(hidden > 0, 1.0, jnp.exp(negative))
    grad_out = (cotangent.astype(jnp.float32) * slope_factor).astype(jnp.bfloat16)
    grad_whole = lax.all_gather(grad_out, "feat", axis=1, tiled=True)
    weight_term = lax.dot_general(
        summed, grad_whole, (((0,), (0,)), ((), ())), preferred_element_type=jnp.float32
    )
    n_feat = lax.axis_size("feat")
    slots = jnp.zeros((n_feat,) + weight_term.shape, jnp.float32)
    slots = lax.dynamic_update_slice_in_dim(slots, weight_term[None], feat_index, 0)
    slots = lax.psum(slots, ("row", "col", "feat"))
    weight_grad = lax.dynamic_index_in_dim(slots, feat_index, 0, keepdims=False) * node_total ** (
        -0.5
    )
    spread = lax.dot_general(
        grad_whole, weight_rows, (((1,), (1,)), ((), ())), preferred_element_type=jnp.float32
    ).astype(jnp.bfloat16)
    spread_panel = lax.all_gather(spread, "col", axis=0, tiled=True)
    spread_blocks = spread_panel.reshape(row_blocks, width, feat_half)[block_rows]
    back_products = jnp.einsum(
        "tji,tjf->tif", local_tiles, spread_blocks, preferred_element_type=jnp.float32
    )
    back_products = back_products * live_mask[:, None, None]
    back_partial = (
        jnp.zeros((col_blocks, width, feat_half), jnp.float32).at[block_cols].add(back_products)
    )
    back_summed = lax.psum_scatter(
        back_partial.reshape(col_blocks * width, feat_half).astype(jnp.bfloat16),
        "row",
        scatter_dimension=0,
        tiled=True,
    )
    return (activated, back_summed, weight_grad)


def solution(mesh):
    return jax.shard_map(
        shards,
        mesh=mesh,
        in_specs=(
            P(("col", "row"), "feat"),
            P("row", "col", None),
            P("row", "col", None),
            P("row", "col"),
            P("row", "col", None, None, None),
            P(),
            P(("row", "col"), "feat"),
        ),
        out_specs=(P(("row", "col"), "feat"), P(("col", "row"), "feat"), P("feat", None)),
        check_vma=False,
    )
```

profile of v0, /device:TPU:2, one launch (start us, length us, event | category | flops | bytes accessed | tf_op | source)
XLA Modules:
  0.0 605.1 jit_solution(15216501221385841070)
XLA Ops:
  9.3 43.2 %all-gather.3.cloned.1.call-done = bf16[8192,128]{1,0:T(8,128)(2,1)} async-done(((bf16[512,128]{1,0:T(8,128)(2,1)}), bf16[8192,128]{1,0:T(8,128)(2,1)}) %all-gather.3.cloned.1.call-update) | async-done | bytes 2097168 | tf_op jit(solution)/shard_map/all_gather | solution.py:22
  52.6 10.2 %gather_fusion = bf16[256,128,128]{2,1,0:T(8,128)(2,1)} fusion(bf16[64,128,128]{2,1,0:T(8,128)(2,1)} %bitcast.36, s32[1024]{0:T(1024)S(1)} %pad_clamp_fusion.1), kind=kCustom, calls=%fused_computation | custom fusion | bytes 16778240 | tf_op jit(solution)/shard_map/gather | solution.py:23
  62.8 13.0 %multiply_bitcast_fusion.1 = f32[256,128,128]{1,2,0:T(8,128)} fusion(bf16[256,128,128]{2,1,0:T(8,128)(2,1)} %gather_fusion, bf16[1,1,256,128,128]{4,3,2,1,0:T(8,128)(2,1)} %param.11, f32[256]{0:T(256)S(1)} %compare_convert_fusion), kind=kOutput, calls=%fused_computation.5 | convolution fusion | flops 1077936128 | bytes 33555456 | tf_op jit(solution)/shard_map/tij,tjf->tif/dot_general | solution.py:24
  75.8 17.4 %copy.17 = f32[256,128,128]{2,1,0:T(8,128)} copy(f32[256,128,128]{1,2,0:T(8,128)} %multiply_bitcast_fusion.1) | data formatting | bytes 33554432 | tf_op jit(solution)/shard_map/mul | solution.py:25
  93.5 33.2 %scatter_fusion = f32[32,128,128]{2,1,0:T(8,128)S(1)} fusion(f32[32,128,128]{2,1,0:T(8,128)S(1)} %broadcast_in_dim.22, s32[256]{0:T(256)S(1)} %bitcast.43, f32[256,128,128]{2,1,0:T(8,128)} %copy.17), kind=kCustom, calls=%fused_computation.2 | custom fusion | flops 4194304 | bytes 50332672 | tf_op jit(solution)/shard_map/scatter-add | solution.py:27
  126.7 1.1 convert_element_type.38
  127.9 74.5 %reduce-scatter.6.cloned.1.call-done = bf16[512,128]{1,0:T(8,128)(2,1)} async-done(((bf16[4096,128]{1,0:T(8,128)(2,1)}), bf16[512,128]{1,0:T(8,128)(2,1)}) %reduce-scatter.6.cloned.1.call-update) | async-done | bytes 131088 | tf_op jit(solution)/shard_map/reduce_scatter | solution.py:29
  202.4 1.1 convolution_convert_fusion
  203.5 0.8 copy.22
  204.4 16.0 %reduce-scatter.10.cloned.1.call-done = bf16[128,512]{1,0:T(8,128)(2,1)} async-done(((bf16[256,512]{1,0:T(8,128)(2,1)}), bf16[128,512]{1,0:T(8,128)(2,1)}) %reduce-scatter.10.cloned.1.call-update) | async-done | bytes 131088
  220.4 1.0 copy.23
  222.3 5.9 all_gather.10
  228.2 0.9 convolution_convert_fusion.1
  229.2 1.1 fusion.2
  231.3 50.6 %all-gather.5.cloned.1.call-done = bf16[4096,128]{1,0:T(8,128)(2,1)} async-done(((bf16[512,128]{1,0:T(8,128)(2,1)}), bf16[4096,128]{1,0:T(8,128)(2,1)}) %all-gather.5.cloned.1.call-update) | async-done | bytes 1048592 | tf_op jit(solution)/shard_map/all_gather | solution.py:58
  281.9 9.8 %gather_fusion.1 = bf16[256,128,128]{2,1,0:T(8,128)(2,1)} fusion(bf16[32,128,128]{2,1,0:T(8,128)(2,1)} %bitcast.35, s32[1024]{0:T(1024)S(1)} %pad_clamp_fusion), kind=kCustom, calls=%fused_computation.1 | custom fusion | bytes 16778240 | tf_op jit(solution)/shard_map/gather | solution.py:59
  291.7 15.4 %multiply_bitcast_fusion = f32[256,128,128]{1,2,0:T(8,128)} fusion(bf16[256,128,128]{2,1,0:T(8,128)(2,1)} %gather_fusion.1, bf16[1,1,256,128,128]{4,3,2,1,0:T(8,128)(2,1)} %param.11, f32[256]{0:T(256)S(1)} %compare_convert_fusion), kind=kOutput, calls=%fused_computation.4 | convolution fusion | flops 1077936128 | bytes 33555456 | tf_op jit(solution)/shard_map/tji,tjf->tif/dot_general | solution.py:60
  307.1 17.5 %copy.19 = f32[256,128,128]{2,1,0:T(8,128)} copy(f32[256,128,128]{1,2,0:T(8,128)} %multiply_bitcast_fusion) | data formatting | bytes 33554432 | tf_op jit(solution)/shard_map/mul | solution.py:63
  324.6 2.5 broadcast_in_dim.23
  327.0 52.1 %scatter_fusion.1 = f32[64,128,128]{2,1,0:T(8,128)} fusion(f32[64,128,128]{2,1,0:T(8,128)} %broadcast_in_dim.23, s32[256]{0:T(256)S(1)} %bitcast.42, f32[256,128,128]{2,1,0:T(8,128)} %copy.19), kind=kCustom, calls=%fused_computation.3 | custom fusion | flops 4194304 | bytes 50332672 | tf_op jit(solution)/shard_map/scatter-add | solution.py:65
  379.1 3.9 convert_element_type.46
  383.1 154.2 %all-reduce.2.cloned.1.call-done = f32[2,128,256]{2,1,0:T(8,128)} async-done(((f32[2,128,256]{2,1,0:T(8,128)}), f32[2,128,256]{2,1,0:T(8,128)}) %all-reduce.2.cloned.1.call-update) | async-done | bytes 262160 | tf_op jit(solution)/shard_map/psum | solution.py:51
  537.3 1.6 multiply_bitcast_fusion.2
  538.8 59.4 %reduce-scatter.8.cloned.1.call-done = bf16[512,128]{1,0:T(8,128)(2,1)} async-done(((bf16[8192,128]{1,0:T(8,128)(2,1)}), bf16[512,128]{1,0:T(8,128)(2,1)}) %reduce-scatter.8.cloned.1.call-update) | async-done | bytes 131088 | tf_op jit(solution)/shard_map/reduce_scatter | solution.py:67
  (27 shorter events, 3.7 us)
Async XLA Ops:
  7.2 195.2 %copy-start = (bf16[256,256]{1,0:T(8,128)(2,1)S(1)}, bf16[256,256]{1,0:T(8,128)(2,1)}, u32[]{:S(2)}) copy-start(bf16[256,256]{1,0:T(8,128)(2,1)} %param.12) | copy-start | bytes 393220
  7.2 45.4 %all-gather.3.cloned.1.call-start = ((), (), s32[]{:S(2)}) async-start(), calls=%async_computation.3 | async-start | bytes 2228224 | tf_op jit(solution)/shard_map/all_gather | solution.py:22
  7.9 194.4 %reduce-scatter.6.cloned.1.call-start = ((), (), s32[]{:S(2)}) async-start(), calls=%async_computation.4 | async-start | bytes 1179648 | tf_op jit(solution)/shard_map/reduce_scatter | solution.py:29
  93.5 128.0 %copy-start.3 = (bf16[512,128]{1,0:T(8,128)(2,1)S(1)}, bf16[512,128]{1,0:T(8,128)(2,1)}, u32[]{:S(2)}) copy-start(bf16[512,128]{1,0:T(8,128)(2,1)} %param.13) | copy-start | bytes 393220
  127.8 92.6 %reduce-scatter.10.cloned.1.call-start = ((), (), s32[]{:S(2)}) async-start(), calls=%async_computation.8 | async-start | bytes 393216
  204.3 77.5 %all-gather.5.cloned.1.call-start = ((), (), s32[]{:S(2)}) async-start(), calls=%async_computation.5 | async-start | bytes 1179648 | tf_op jit(solution)/shard_map/all_gather | solution.py:58
  229.1 308.2 %all-reduce.2.cloned.1.call-start = ((), (), s32[]{:S(2)}) async-start(), calls=%async_computation.7 | async-start | bytes 524288 | tf_op jit(solution)/shard_map/psum | solution.py:51
  230.3 0.7 copy-start.2
  231.0 367.2 %reduce-scatter.8.cloned.1.call-start = ((), (), s32[]{:S(2)}) async-start(), calls=%async_computation.6 | async-start | bytes 2228224 | tf_op jit(solution)/shard_map/reduce_scatter | solution.py:67
  327.0 271.2 %copy-start.1 = (bf16[256,256]{1,0:T(8,128)(2,1)S(1)}, bf16[256,256]{1,0:T(8,128)(2,1)}, u32[]{:S(2)}) copy-start(bf16[256,256]{1,0:T(8,128)(2,1)} %param.12) | copy-start | bytes 393220
Sparse Core Ops, SparseCore 0:
  9.8 42.6 all-gather.2
  127.9 74.3 reduce-scatter.5
  205.0 15.3 reduce-scatter.9
  229.2 52.6 all-gather.4
  287.2 250.0 all-reduce.1
  540.2 57.9 reduce-scatter.7
where the time goes:
time: 607 us; the launch traced here: 605 us
  waiting for transfers between devices  399 us (66%)
  other arithmetic  93.4 us (15%)
  local copies, waits for them, and re-layouts  60.2 us (10%)
  matrix products  31.5 us (5%)
  between operations  14.9 us (2%)
    psum x1, waiting for transfers between devices, shards(): slots = lax.psum(slots, ('row', 'col', 'feat'))  154 us
    reduce_scatter x1, waiting for transfers between devices, shards(): lax.psum_scatter(partial_value.reshape(row_blocks * width, feat_half).ast...  74.5 us
    reduce_scatter x1, waiting for transfers between devices, shards(): lax.psum_scatter(back_partial.reshape(col_blocks * width, feat_half).asty...  59.4 us
    scatter-add x1, other arithmetic, shards(): jnp.zeros((col_blocks, width, feat_half), jnp.float32).at[block_cols]  52.1 us
    all_gather x1, waiting for transfers between devices, shards(): spread_panel = lax.all_gather(spread, 'col', axis=0, tiled=True)  50.6 us
    all_gather x1, waiting for transfers between devices, shards(): panel = lax.all_gather(features, 'row', axis=0, tiled=True)  43.2 us
    scatter-add x1, other arithmetic, shards(): jnp.zeros((row_blocks, width, feat_half), jnp.float32).at[block_rows]  33.2 us
    mul x1, local copies, waits for them, and re-layouts, shards(): back_products = back_products * live_mask[:, None, None]  17.5 us
  transfers between devices with their start and end apart: 6, of which 6 were waited for; matrix products, arithmetic and copies ran while one was open for 17% of the time, Pallas kernels for 0%

commit v1 on v0

--- a/solution.py
+++ b/solution.py
@@ -19,7 +19,16 @@
     row_blocks = local_blocks * n_coldev
     col_blocks = local_blocks * n_rowdev
     node_total = features.shape[0] * n_rowdev * n_coldev
-    panel = lax.all_gather(features, "row", axis=0, tiled=True)
+    ways = lax.axis_size("row")
+    up = [(d, (d + 1) % ways) for d in range(ways)]
+    down = [(d, (d - 1) % ways) for d in range(ways)]
+    earlier, later = ([features], [features])
+    for _ in range(ways // 2):
+        earlier.append(lax.ppermute(earlier[-1], "row", up))
+    for _ in range((ways - 1) // 2):
+        later.append(lax.ppermute(later[-1], "row", down))
+    line = jnp.concatenate([*earlier[::-1], *later[1:]], axis=0)
+    panel = jnp.roll(line, (lax.axis_index("row") - ways // 2) * features.shape[0], axis=0)
     gathered = panel.reshape(col_blocks, width, feat_half)[block_cols]
     products = jnp.einsum("tij,tjf->tif", local_tiles, gathered, preferred_element_type=jnp.float32)
     products = products * live_mask[:, None, None]

time: 607 us -> 611 us (level)
  starting transfers between devices: 0.42 us -> 21.5 us
  waiting for transfers between devices: 399 us -> 382 us
    all_gather x1 -> x0, waiting for transfers between devices: 43.2 us -> none  [shards(): panel = lax.all_gather(features, 'row', axis=0, tiled=True)]
    ppermute x0 -> x15, waiting for transfers between devices: none -> 24.9 us  [the longest x8 24 us: shards(): earlier.append(lax.ppermute(earlier[-1], 'row', up))]
    ppermute x0 -> x15, starting transfers between devices: none -> 21.1 us  [the longest x7 21.1 us: shards(): later.append(lax.ppermute(later[-1], 'row', down))]
    unnamed x7 -> x6, waiting for transfers between devices: 16.8 us -> 16.1 us
  transfers between devices with their start and end apart: 6 -> 20, of which waited for: 6 -> 17; matrix products, arithmetic and copies ran while one was open for 17% -> 17% of each run, Pallas kernels for 0% -> 0%
where the time goes in v1:
time: 611 us; the launch traced here: 610 us
  waiting for transfers between devices  382 us (63%)
  other arithmetic  93.1 us (15%)
  local copies, waits for them, and re-layouts  60.3 us (10%)
  matrix products  31.6 us (5%)
  starting transfers between devices  21.5 us (4%)
  between operations  14.8 us (2%)
    psum x1, waiting for transfers between devices, shards(): slots = lax.psum(slots, ('row', 'col', 'feat'))  154 us
    reduce_scatter x1, waiting for transfers between devices, shards(): lax.psum_scatter(partial_value.reshape(row_blocks * width, feat_half).ast...  76.7 us
    reduce_scatter x1, waiting for transfers between devices, shards(): lax.psum_scatter(back_partial.reshape(col_blocks * width, feat_half).asty...  59.4 us
    scatter-add x1, other arithmetic, shards(): jnp.zeros((col_blocks, width, feat_half), jnp.float32).at[block_cols]  51.8 us
    all_gather x1, waiting for transfers between devices, shards(): spread_panel = lax.all_gather(spread, 'col', axis=0, tiled=True)  50.6 us
    scatter-add x1, other arithmetic, shards(): jnp.zeros((row_blocks, width, feat_half), jnp.float32).at[block_rows]  33.2 us
    ppermute x8, waiting for transfers between devices, shards(): earlier.append(lax.ppermute(earlier[-1], 'row', up))  24 us
    ppermute x7, starting transfers between devices, shards(): later.append(lax.ppermute(later[-1], 'row', down))  21.1 us
  transfers between devices with their start and end apart: 20, of which 17 were waited for; matrix products, arithmetic and copies ran while one was open for 17% of the time, Pallas kernels for 0%

profile of v1, /device:TPU:2, one launch (start us, length us, event | category | flops | bytes accessed | tf_op | source)
XLA Modules:
  0.0 609.5 jit_solution(36887731074195980)
XLA Ops:
  7.3 8.1 %collective-permute-done = bf16[512,128]{1,0:T(8,128)(2,1)S(1)} collective-permute-done((bf16[512,128]{1,0:T(8,128)(2,1)}, bf16[512,128]{1,0:T(8,128)(2,1)S(1)}, u32[]{:S(2)}, u32[]{:S(2)}) %collective-permute-start) | collective-permute-done | bytes 131104 | tf_op jit(solution)/shard_map/ppermute | solution.py:27
  15.4 3.0 collective-permute-start.8
  18.4 2.6 collective-permute-done.1
  21.2 3.0 collective-permute-start.9
  26.7 3.1 collective-permute-start.10
  32.3 3.1 collective-permute-start.11
  38.5 3.0 collective-permute-start.12
  44.1 3.0 collective-permute-start.13
  49.6 3.1 collective-permute-start.14
  56.6 8.6 %gather_fusion = bf16[256,128,128]{2,1,0:T(8,128)(2,1)} fusion(bf16[64,128,128]{2,1,0:T(8,128)(2,1)S(1)} %bitcast.36, s32[1024]{0:T(1024)S(1)} %pad_clamp_fusion.1), kind=kCustom, calls=%fused_computation | custom fusion | bytes 16778240 | tf_op jit(solution)/shard_map/gather | solution.py:32
  65.2 13.0 %multiply_bitcast_fusion.1 = f32[256,128,128]{1,2,0:T(8,128)} fusion(bf16[256,128,128]{2,1,0:T(8,128)(2,1)} %gather_fusion, bf16[1,1,256,128,128]{4,3,2,1,0:T(8,128)(2,1)} %param.11, f32[256]{0:T(256)S(1)} %compare_convert_fusion), kind=kOutput, calls=%fused_computation.5 | convolution fusion | flops 1077936128 | bytes 33555456 | tf_op jit(solution)/shard_map/tij,tjf->tif/dot_general | solution.py:33
  78.2 17.5 %copy.17 = f32[256,128,128]{2,1,0:T(8,128)} copy(f32[256,128,128]{1,2,0:T(8,128)} %multiply_bitcast_fusion.1) | data formatting | bytes 33554432 | tf_op jit(solution)/shard_map/mul | solution.py:34
  95.9 33.2 %scatter_fusion = f32[32,128,128]{2,1,0:T(8,128)S(1)} fusion(f32[32,128,128]{2,1,0:T(8,128)S(1)} %broadcast_in_dim.22, s32[256]{0:T(256)S(1)} %bitcast.43, f32[256,128,128]{2,1,0:T(8,128)} %copy.17), kind=kCustom, calls=%fused_computation.2 | custom fusion | flops 4194304 | bytes 50332672 | tf_op jit(solution)/shard_map/scatter-add | solution.py:36
  130.4 76.7 %reduce-scatter.6.cloned.1.call-done = bf16[512,128]{1,0:T(8,128)(2,1)} async-done(((bf16[4096,128]{1,0:T(8,128)(2,1)}), bf16[512,128]{1,0:T(8,128)(2,1)}) %reduce-scatter.6.cloned.1.call-update) | async-done | bytes 131088 | tf_op jit(solution)/shard_map/reduce_scatter | solution.py:38
  209.1 16.0 %reduce-scatter.10.cloned.1.call-done = bf16[128,512]{1,0:T(8,128)(2,1)} async-done(((bf16[256,512]{1,0:T(8,128)(2,1)}), bf16[128,512]{1,0:T(8,128)(2,1)}) %reduce-scatter.10.cloned.1.call-update) | async-done | bytes 131088
  227.0 5.9 all_gather.6
  236.0 50.6 %all-gather.2.cloned.1.call-done = bf16[4096,128]{1,0:T(8,128)(2,1)} async-done(((bf16[512,128]{1,0:T(8,128)(2,1)}), bf16[4096,128]{1,0:T(8,128)(2,1)}) %all-gather.2.cloned.1.call-update) | async-done | bytes 1048592 | tf_op jit(solution)/shard_map/all_gather | solution.py:67
  286.6 9.8 %gather_fusion.1 = bf16[256,128,128]{2,1,0:T(8,128)(2,1)} fusion(bf16[32,128,128]{2,1,0:T(8,128)(2,1)} %bitcast.35, s32[1024]{0:T(1024)S(1)} %pad_clamp_fusion), kind=kCustom, calls=%fused_computation.1 | custom fusion | bytes 16778240 | tf_op jit(solution)/shard_map/gather | solution.py:68
  296.4 15.4 %multiply_bitcast_fusion = f32[256,128,128]{1,2,0:T(8,128)} fusion(bf16[256,128,128]{2,1,0:T(8,128)(2,1)} %gather_fusion.1, bf16[1,1,256,128,128]{4,3,2,1,0:T(8,128)(2,1)} %param.11, f32[256]{0:T(256)S(1)} %compare_convert_fusion), kind=kOutput, calls=%fused_computation.4 | convolution fusion | flops 1077936128 | bytes 33555456 | tf_op jit(solution)/shard_map/tji,tjf->tif/dot_general | solution.py:69
  311.8 17.5 %copy.19 = f32[256,128,128]{2,1,0:T(8,128)} copy(f32[256,128,128]{1,2,0:T(8,128)} %multiply_bitcast_fusion) | data formatting | bytes 33554432 | tf_op jit(solution)/shard_map/mul | solution.py:72
  331.8 51.8 %scatter_fusion.1 = f32[64,128,128]{2,1,0:T(8,128)} fusion(f32[64,128,128]{2,1,0:T(8,128)} %broadcast_in_dim.23, s32[256]{0:T(256)S(1)} %bitcast.42, f32[256,128,128]{2,1,0:T(8,128)} %copy.19), kind=kCustom, calls=%fused_computation.3 | custom fusion | flops 4194304 | bytes 50332672 | tf_op jit(solution)/shard_map/scatter-add | solution.py:74
  383.6 3.9 convert_element_type.46
  387.5 154.5 %all-reduce.2.cloned.1.call-done = f32[2,128,256]{2,1,0:T(8,128)} async-done(((f32[2,128,256]{2,1,0:T(8,128)}), f32[2,128,256]{2,1,0:T(8,128)}) %all-reduce.2.cloned.1.call-update) | async-done | bytes 262160 | tf_op jit(solution)/shard_map/psum | solution.py:60
  543.6 59.4 %reduce-scatter.8.cloned.1.call-done = bf16[512,128]{1,0:T(8,128)(2,1)} async-done(((bf16[8192,128]{1,0:T(8,128)(2,1)}), bf16[512,128]{1,0:T(8,128)(2,1)}) %reduce-scatter.8.cloned.1.call-update) | async-done | bytes 131088 | tf_op jit(solution)/shard_map/reduce_scatter | solution.py:76
  (89 shorter events, 28.9 us)
Async XLA Ops:
  7.2 199.9 %copy-start = (bf16[256,256]{1,0:T(8,128)(2,1)S(1)}, bf16[256,256]{1,0:T(8,128)(2,1)}, u32[]{:S(2)}) copy-start(bf16[256,256]{1,0:T(8,128)(2,1)} %param.12) | copy-start | bytes 393220
  7.2 49.0 %copy-start.3 = (bf16[512,128]{1,0:T(8,128)(2,1)S(1)}, bf16[512,128]{1,0:T(8,128)(2,1)}, u32[]{:S(2)}) copy-start(bf16[512,128]{1,0:T(8,128)(2,1)} %param.7) | copy-start | bytes 393220
  7.2 199.9 %reduce-scatter.6.cloned.1.call-start = ((), (), s32[]{:S(2)}) async-start(), calls=%async_computation.3 | async-start | bytes 1179648 | tf_op jit(solution)/shard_map/reduce_scatter | solution.py:38
  7.2 8.2 %collective-permute-start = (bf16[512,128]{1,0:T(8,128)(2,1)}, bf16[512,128]{1,0:T(8,128)(2,1)S(1)}, u32[]{:S(2)}, u32[]{:S(2)}) collective-permute-start(bf16[512,128]{1,0:T(8,128)(2,1)} %param.7), channel_id=1, source_target_pairs={{0,16},{16,32},{32,48},{48,64},{64,80},{80,96},{96,112},{112,128},... | collective-permute-start | bytes 393224 | tf_op jit(solution)/shard_map/ppermute | solution.py:27
  15.4 5.6 collective-permute-start.1
  15.4 5.8 collective-permute-start.8
  21.0 5.6 collective-permute-start.2
  21.2 5.5 collective-permute-start.9
  26.6 5.6 collective-permute-start.3
  26.7 5.6 collective-permute-start.10
  32.2 5.6 collective-permute-start.4
  32.3 6.2 %collective-permute-start.11 = (bf16[512,128]{1,0:T(8,128)(2,1)S(1)}, bf16[512,128]{1,0:T(8,128)(2,1)S(1)}, u32[]{:S(2)}, u32[]{:S(2)}) collective-permute-start(bf16[512,128]{1,0:T(8,128)(2,1)S(1)} %collective-permute-done.10), channel_id=1, source_target_pairs={{0,240},{16,0},{32,16},{48,32},{64,48},{80,64},{96,80},{112,96},{1... | collective-permute-start | bytes 393224 | tf_op jit(solution)/shard_map/ppermute | solution.py:29
  37.8 5.6 collective-permute-start.5
  38.5 5.6 collective-permute-start.12
  43.4 5.6 collective-permute-start.6
  44.1 5.5 collective-permute-start.13
  49.0 5.6 collective-permute-start.7
  49.6 6.3 %collective-permute-start.14 = (bf16[512,128]{1,0:T(8,128)(2,1)S(1)}, bf16[512,128]{1,0:T(8,128)(2,1)S(1)}, u32[]{:S(2)}, u32[]{:S(2)}) collective-permute-start(bf16[512,128]{1,0:T(8,128)(2,1)S(1)} %collective-permute-done.13), channel_id=1, source_target_pairs={{0,240},{16,0},{32,16},{48,32},{64,48},{80,64},{96,80},{112,96},{1... | collective-permute-start | bytes 393224 | tf_op jit(solution)/shard_map/ppermute | solution.py:29
  129.1 97.0 %copy-start.4 = (bf16[512,128]{1,0:T(8,128)(2,1)S(1)}, bf16[512,128]{1,0:T(8,128)(2,1)}, u32[]{:S(2)}) copy-start(bf16[512,128]{1,0:T(8,128)(2,1)} %param.13) | copy-start | bytes 393220
  130.3 94.8 %reduce-scatter.10.cloned.1.call-start = ((), (), s32[]{:S(2)}) async-start(), calls=%async_computation.7 | async-start | bytes 393216
  209.1 77.5 %all-gather.2.cloned.1.call-start = ((), (), s32[]{:S(2)}) async-start(), calls=%async_computation.4 | async-start | bytes 1179648 | tf_op jit(solution)/shard_map/all_gather | solution.py:67
  233.8 308.2 %all-reduce.2.cloned.1.call-start = ((), (), s32[]{:S(2)}) async-start(), calls=%async_computation.6 | async-start | bytes 524288 | tf_op jit(solution)/shard_map/psum | solution.py:60
  235.8 367.2 %reduce-scatter.8.cloned.1.call-start = ((), (), s32[]{:S(2)}) async-start(), calls=%async_computation.5 | async-start | bytes 2228224 | tf_op jit(solution)/shard_map/reduce_scatter | solution.py:76
  331.8 271.2 %copy-start.1 = (bf16[256,256]{1,0:T(8,128)(2,1)S(1)}, bf16[256,256]{1,0:T(8,128)(2,1)}, u32[]{:S(2)}) copy-start(bf16[256,256]{1,0:T(8,128)(2,1)} %param.12) | copy-start | bytes 393220
  (1 other events, 0.7 us)
Sparse Core Ops, SparseCore 0:
  130.4 76.6 reduce-scatter.5
  209.7 15.3 reduce-scatter.9
  233.9 52.6 all-gather.1
  291.9 250.0 all-reduce.1
  544.9 57.9 reduce-scatter.7
